TPU v7x, 512 devices: a whole 4x8x8 slice. The times are simulated.
512 devices in a mesh: ao: 32 (over x, z), ri: 16 (over y, core).
Axes of the slice: x: 4, y: 8, z: 8, core: 2. Of those that a mesh axis runs over, the one named last changes fastest.
Arguments:
- three_center: bfloat16 [256, 12288, 128], P('ri', 'ao'), may hold values from -0.19921875 to 0.19921875
- occ_band: bfloat16 [4096, 640], P('ao'), may hold values from -0.3125 to 0.3125
- virt_band: bfloat16 [4096, 384], P('ao'), may hold values from -0.3125 to 0.3125
- three_mask: int32 [32, 3], P('ao'), may hold values 0 or 1
- occ_mask: int32 [32, 5], P('ao'), may hold values 0 or 1
- virt_mask: int32 [32, 3], P('ao'), may hold values 0 or 1
Outputs:
- chi: float32 [256, 256], P('ri')
All inputs are finite; a program needn't handle non-finite values. No bound on the sum of `three_mask` or of `occ_mask` or of `virt_mask` on one device may be relied on, other than what follows from the above.
Results may differ from a plain program's by a relative error of at most 0.004.
Values may be sent and summed in bfloat16 or wider, within the bound.
A program may use at most 64 MiB of HBM per device.

v0:
```python
import jax
import jax.numpy as jnp
from jax import lax
from jax.sharding import PartitionSpec as P


def padded_2(value, sides, width):
    for axis, dim in sides:
        peers, length = (lax.axis_size(axis), value.shape[dim])
        up = [(i, (i + 1) % peers) for i in range(peers)]
        down = [(j, i) for i, j in up]
        last = lax.slice_in_dim(value, length - width, length, axis=dim)
        initial = lax.slice_in_dim(value, 0, width, axis=dim)
        before = lax.ppermute(last, axis, up)
        after = lax.ppermute(initial, axis, down)
        value = jnp.concatenate([before, value, after], axis=dim)
    return value


def per_device(three_center, occ_band, virt_band, three_mask, occ_mask, virt_mask):
    tile_size = occ_band.shape[0]
    local_rows = three_center.shape[0]
    live_b = (
        three_center.reshape(local_rows, 3, tile_size, tile_size)
        * three_mask[0].astype(three_center.dtype)[None, :, None, None]
    )
    live_b = live_b.reshape(local_rows, 3 * tile_size, tile_size)
    live_occ = occ_band * jnp.repeat(occ_mask[0].astype(occ_band.dtype), tile_size)[None, :]
    live_virt = virt_band * jnp.repeat(virt_mask[0].astype(virt_band.dtype), tile_size)[None, :]
    occ_rows = padded_2(live_occ, (("ao", 0),), tile_size)
    blank = jnp.zeros((tile_size, tile_size), occ_band.dtype)
    green_block = jnp.concatenate(
        [
            jnp.concatenate([occ_rows[0:tile_size, tile_size:], blank], 1),
            occ_rows[tile_size : 2 * tile_size],
            jnp.concatenate([blank, occ_rows[2 * tile_size :, : 4 * tile_size]], 1),
        ],
        0,
    )
    m_local = jnp.einsum(
        "ml,pmn->pln", green_block, live_b, preferred_element_type=jnp.float32
    ).astype(jnp.bfloat16)
    padded = padded_2(m_local, (("ao", 2),), tile_size)
    needed = jnp.concatenate(
        [
            padded[:, 2 * tile_size : 5 * tile_size, 0:tile_size],
            padded[:, tile_size : 4 * tile_size, tile_size : 2 * tile_size],
            padded[:, 0 : 3 * tile_size, 2 * tile_size : 3 * tile_size],
        ],
        2,
    )
    product = jnp.einsum(
        "plv,sv->pls", needed, live_virt, preferred_element_type=jnp.float32
    ).astype(jnp.bfloat16)
    product_flat = product.reshape(local_rows, 3 * tile_size * tile_size)
    b_flat = live_b.reshape(local_rows, 3 * tile_size * tile_size)
    product_all, b_all = (
        lax.all_to_all(product_flat, "ri", split_axis=1, concat_axis=0, tiled=True),
        lax.all_to_all(b_flat, "ri", split_axis=1, concat_axis=0, tiled=True),
    )
    partial_chi = lax.dot_general(
        product_all, b_all, (((1,), (1,)), ((), ())), preferred_element_type=jnp.float32
    )
    row_panel = lax.psum_scatter(partial_chi, "ri", scatter_dimension=0, tiled=True)
    summed = lax.psum(row_panel, "ao")
    return -summed


def solution(mesh):
    placed = (
        P("ri", "ao", None),
        P("ao", None),
        P("ao", None),
        P("ao", None),
        P("ao", None),
        P("ao", None),
    )
    return jax.shard_map(
        per_device, mesh=mesh, in_specs=placed, out_specs=P("ri", None), check_vma=False
    )
```

profile of v0, /device:TPU:32, one launch (start us, length us, event | category | flops | bytes accessed | tf_op | source)
XLA Modules:
  0.0 353.9 jit_solution(3540133267525671056)
XLA Ops:
  6.5 0.7 convert_bitcast_fusion.2
  7.2 0.1 broadcast_bitcast_fusion
  7.3 0.9 broadcast_multiply_fusion.1
  8.2 4.3 %collective-permute-start = (bf16[128,640]{1,0:T(8,128)(2,1)S(1)}, bf16[128,640]{1,0:T(8,128)(2,1)}, u32[]{:S(2)}, u32[]{:S(2)}) collective-permute-start(bf16[128,640]{1,0:T(8,128)(2,1)S(1)} %broadcast_multiply_fusion.1), channel_id=1, source_target_pairs={{0,16},{16,32},{32,48},{48,64},{64,80},{80,96},{96,112},{112,128},... | collective-permute-start | bytes 491528 | tf_op jit(solution)/shard_map/ppermute | solution.py:14
  12.5 10.8 %collective-permute-start.1 = (bf16[128,640]{1,0:T(8,128)(2,1)S(1)}, bf16[128,640]{1,0:T(8,128)(2,1)}, u32[]{:S(2)}, u32[]{:S(2)}) collective-permute-start(bf16[128,640]{1,0:T(8,128)(2,1)S(1)} %broadcast_multiply_fusion.1), channel_id=1, source_target_pairs={{16,0},{32,16},{48,32},{64,48},{80,64},{96,80},{112,96},{128,112},... | collective-permute-start | bytes 491528 | tf_op jit(solution)/shard_map/ppermute | solution.py:15
  23.3 0.7 convert_bitcast_fusion.3
  23.9 0.1 mul.53
  24.1 0.0 copy-start
  24.1 2.7 reshape.31
  26.8 0.1 broadcast_bitcast_fusion.2
  26.9 0.0 collective-permute-done
  26.9 0.9 slice.20
  27.8 0.0 collective-permute-done.1
  27.8 0.9 slice.21
  28.7 0.0 copy-done
  28.7 3.3 convert_bitcast_fusion
  32.0 1.9 collective-permute-start.2
  34.0 7.2 %collective-permute-start.3 = (bf16[16,640,128]{1,2,0:T(8,128)(2,1)}, bf16[16,640,128]{1,2,0:T(8,128)(2,1)}, u32[]{:S(2)}, u32[]{:S(2)}) collective-permute-start(bf16[16,640,128]{1,2,0:T(8,128)(2,1)} %convert_bitcast_fusion), channel_id=1, source_target_pairs={{16,0},{32,16},{48,32},{64,48},{80,64},{96,80},{112,96},{128,112},... | collective-permute-start | bytes 7864328 | tf_op jit(solution)/shard_map/ppermute | solution.py:15
  41.2 0.1 broadcast_multiply_fusion
  41.3 2.0 copy.19
  43.4 0.0 copy-start.2
  43.4 7.4 %all-to-all-start.1 = ((bf16[16,16,3072]{2,0,1:T(8,128)(2,1)}), bf16[16,16,3072]{2,0,1:T(8,128)(2,1)}, u32[]{:S(2)}, u32[]{:S(2)}) async-start(bf16[16,16,3072]{2,0,1:T(8,128)(2,1)} %copy.19), calls=%async_computation.1 | async-start | bytes 3145728 | tf_op jit(solution)/shard_map/all_to_all | solution.py:59
  50.7 0.0 reduce-scatter.2.cloned.1.call-start
  50.8 0.0 copy-done.2
  50.8 0.1 broadcast_bitcast_fusion.1
  50.9 1.6 slice.23
  52.5 43.4 %collective-permute-done.2 = bf16[16,640,128]{1,2,0:T(8,128)(2,1)} collective-permute-done((bf16[16,640,128]{1,2,0:T(8,128)(2,1)}, bf16[16,640,128]{1,2,0:T(8,128)(2,1)}, u32[]{:S(2)}, u32[]{:S(2)}) %collective-permute-start.2) | collective-permute-done | bytes 2621472 | tf_op jit(solution)/shard_map/ppermute | solution.py:14
  95.9 1.6 slice.22
  97.5 0.0 copy-start.1
  97.5 0.0 collective-permute-done.3
  97.5 1.6 slice.24
  99.1 0.0 copy-done.1
  99.2 1.7 fusion.6
  100.8 0.7 all_to_all.26
  101.5 0.9 copy.18
  102.4 0.0 all-to-all-done.1
  102.4 42.5 %all_to_all.35 = bf16[16,16,3072]{2,0,1:T(8,128)(2,1)S(1)} all-to-all(bf16[16,16,3072]{2,0,1:T(8,128)(2,1)S(1)} %copy.18), channel_id=1, replica_groups=mesh['ao'=32,'ri'=16] {'ri'}, dimensions={1} | all-to-all | bytes 3145728 | tf_op jit(solution)/shard_map/all_to_all | solution.py:58
  144.9 2.7 fusion.32
  147.6 0.0 reduce-scatter.2.cloned.1.call-update
  147.6 55.1 %reduce-scatter.2.cloned.1.call-done = f32[16,256]{1,0:T(8,128)} async-done(((f32[256,256]{1,0:T(8,128)}), f32[16,256]{1,0:T(8,128)}) %reduce-scatter.2.cloned.1.call-update) | async-done | bytes 16400 | tf_op jit(solution)/shard_map/reduce_scatter | solution.py:64
  202.8 143.7 %psum.7 = f32[16,256]{1,0:T(8,128)S(1)} all-reduce(f32[16,256]{1,0:T(8,128)} %reduce-scatter.2.cloned.1.call-done), channel_id=1, replica_groups=mesh['ao'=32,'ri'=16] {'ao'}, use_global_device_ids=true, to_apply=%region_1.0 | all-reduce | flops 4096 | bytes 32768 | tf_op jit(solution)/shard_map/psum | solution.py:65
  346.5 0.6 neg.3
  (2 shorter events, 0.1 us)
Async XLA Ops:
  8.2 18.7 %collective-permute-start = (bf16[128,640]{1,0:T(8,128)(2,1)S(1)}, bf16[128,640]{1,0:T(8,128)(2,1)}, u32[]{:S(2)}, u32[]{:S(2)}) collective-permute-start(bf16[128,640]{1,0:T(8,128)(2,1)S(1)} %broadcast_multiply_fusion.1), channel_id=1, source_target_pairs={{0,16},{16,32},{32,48},{48,64},{64,80},{80,96},{96,112},{112,128},... | collective-permute-start | bytes 491528 | tf_op jit(solution)/shard_map/ppermute | solution.py:14
  12.5 15.3 %collective-permute-start.1 = (bf16[128,640]{1,0:T(8,128)(2,1)S(1)}, bf16[128,640]{1,0:T(8,128)(2,1)}, u32[]{:S(2)}, u32[]{:S(2)}) collective-permute-start(bf16[128,640]{1,0:T(8,128)(2,1)S(1)} %broadcast_multiply_fusion.1), channel_id=1, source_target_pairs={{16,0},{32,16},{48,32},{64,48},{80,64},{96,80},{112,96},{128,112},... | collective-permute-start | bytes 491528 | tf_op jit(solution)/shard_map/ppermute | solution.py:15
  24.1 4.6 %copy-start = (bf16[16,384,128]{2,1,0:T(8,128)(2,1)S(1)}, bf16[16,384,128]{2,1,0:T(8,128)(2,1)}, u32[]{:S(2)}) copy-start(bf16[16,384,128]{2,1,0:T(8,128)(2,1)} %param.6) | copy-start | bytes 4718596
  32.0 63.8 %collective-permute-start.2 = (bf16[16,640,128]{1,2,0:T(8,128)(2,1)}, bf16[16,640,128]{1,2,0:T(8,128)(2,1)}, u32[]{:S(2)}, u32[]{:S(2)}) collective-permute-start(bf16[16,640,128]{1,2,0:T(8,128)(2,1)} %convert_bitcast_fusion), channel_id=1, source_target_pairs={{0,16},{16,32},{32,48},{48,64},{64,80},{80,96},{96,112},{112,128},... | collective-permute-start | bytes 7864328 | tf_op jit(solution)/shard_map/ppermute | solution.py:14
  34.0 63.5 %collective-permute-start.3 = (bf16[16,640,128]{1,2,0:T(8,128)(2,1)}, bf16[16,640,128]{1,2,0:T(8,128)(2,1)}, u32[]{:S(2)}, u32[]{:S(2)}) collective-permute-start(bf16[16,640,128]{1,2,0:T(8,128)(2,1)} %convert_bitcast_fusion), channel_id=1, source_target_pairs={{16,0},{32,16},{48,32},{64,48},{80,64},{96,80},{112,96},{128,112},... | collective-permute-start | bytes 7864328 | tf_op jit(solution)/shard_map/ppermute | solution.py:15
  43.4 7.4 %copy-start.2 = (s32[1,3]{1,0:T(1,128)S(1)}, s32[1,3]{1,0:T(1,128)}, u32[]{:S(2)}) copy-start(s32[1,3]{1,0:T(1,128)} %param.11) | copy-start | bytes 40
  43.4 59.0 %all-to-all-start.1 = ((bf16[16,16,3072]{2,0,1:T(8,128)(2,1)}), bf16[16,16,3072]{2,0,1:T(8,128)(2,1)}, u32[]{:S(2)}, u32[]{:S(2)}) async-start(bf16[16,16,3072]{2,0,1:T(8,128)(2,1)} %copy.19), calls=%async_computation.1 | async-start | bytes 3145728 | tf_op jit(solution)/shard_map/all_to_all | solution.py:59
  50.7 152.0 %reduce-scatter.2.cloned.1.call-start = ((), (), s32[]{:S(2)}) async-start(), calls=%async_computation.3 | async-start | bytes 278528 | tf_op jit(solution)/shard_map/reduce_scatter | solution.py:64
  97.5 1.7 copy-start.1
Sparse Core Ops, SparseCore 0:
  147.8 54.9 reduce-scatter.1
where the time goes:
time: 354 us
  blocking collectives  186 us (53%)
  waiting for transfers between devices  98.6 us (28%)
  starting transfers between devices  31.6 us (9%)
  between operations  13.6 us (4%)
  local copies, waits for them, and re-layouts  13.3 us (4%)
  matrix products  7.72 us (2%)
    psum x1, blocking collectives, per_device(): summed = lax.psum(row_panel, 'ao')  144 us
    reduce_scatter x1, waiting for transfers between devices, per_device(): lax.psum_scatter(partial_chi, 'ri', scatter_dimension=0, tiled=True)  55.1 us
    ppermute x2, waiting for transfers between devices, padded_2(): before = lax.ppermute(last, axis, up)  43.4 us
    all_to_all x1, blocking collectives, per_device(): lax.all_to_all(product_flat, 'ri', split_axis=1, concat_axis=0, tiled=True)  42.5 us
    ppermute x2, starting transfers between devices, padded_2(): after = lax.ppermute(initial, axis, down)  18 us
    all_to_all x1, starting transfers between devices, per_device(): lax.all_to_all(b_flat, 'ri', split_axis=1, concat_axis=0, tiled=True)  7.36 us
  transfers between devices with their start and end apart: 6, of which 2 were waited for; matrix products, arithmetic and copies ran while one was open for 4% of the time, Pallas kernels for 0%

commit v1 on v0

--- a/solution.py
+++ b/solution.py
@@ -62,7 +62,7 @@
         product_all, b_all, (((1,), (1,)), ((), ())), preferred_element_type=jnp.float32
     )
     row_panel = lax.psum_scatter(partial_chi, "ri", scatter_dimension=0, tiled=True)
-    summed = lax.psum(row_panel, "ao")
+    summed = jnp.sum(lax.all_gather(row_panel, "ao"), axis=0)
     return -summed
 
 

time: 354 us -> 264 us (0.75)
  the two profiles are of different devices: /device:TPU:32 before, /device:TPU:2 now
where the time goes in v1:
time: 264 us; the launch traced here: 263 us
  waiting for transfers between devices  102 us (39%)
  blocking collectives  95.6 us (36%)
  starting transfers between devices  28.2 us (11%)
  between operations  13.6 us (5%)
  local copies, waits for them, and re-layouts  13.3 us (5%)
  matrix products  7.72 us (3%)
  other arithmetic  3.03 us (1%)
    reduce_scatter x1, waiting for transfers between devices, per_device(): lax.psum_scatter(partial_chi, 'ri', scatter_dimension=0, tiled=True)  58.4 us
    all_gather x1, blocking collectives, per_device(): summed = jnp.sum(lax.all_gather(row_panel, 'ao'), axis=0)  50.2 us
    all_to_all x1, blocking collectives, per_device(): lax.all_to_all(product_flat, 'ri', split_axis=1, concat_axis=0, tiled=True)  45.4 us
    ppermute x2, waiting for transfers between devices, padded_2(): before = lax.ppermute(last, axis, up)  43.4 us
    ppermute x2, starting transfers between devices, padded_2(): after = lax.ppermute(initial, axis, down)  14.6 us
    all_to_all x1, starting transfers between devices, per_device(): lax.all_to_all(b_flat, 'ri', split_axis=1, concat_axis=0, tiled=True)  7.38 us
    ppermute x2, starting transfers between devices, padded_2(): before = lax.ppermute(last, axis, up)  6.19 us
  transfers between devices with their start and end apart: 6, of which 2 were waited for; matrix products, arithmetic and copies ran while one was open for 5% of the time, Pallas kernels for 0%

profile of v1, /device:TPU:2, one launch (start us, length us, event | category | flops | bytes accessed | tf_op | source)
XLA Modules:
  0.0 263.3 jit_solution(7124894878028157576)
XLA Ops:
  6.5 0.7 convert_bitcast_fusion.2
  7.2 0.1 broadcast_bitcast_fusion
  7.3 0.9 broadcast_multiply_fusion.1
  8.2 4.3 %collective-permute-start = (bf16[128,640]{1,0:T(8,128)(2,1)S(1)}, bf16[128,640]{1,0:T(8,128)(2,1)}, u32[]{:S(2)}, u32[]{:S(2)}) collective-permute-start(bf16[128,640]{1,0:T(8,128)(2,1)S(1)} %broadcast_multiply_fusion.1), channel_id=1, source_target_pairs={{0,16},{16,32},{32,48},{48,64},{64,80},{80,96},{96,112},{112,128},... | collective-permute-start | bytes 491528 | tf_op jit(solution)/shard_map/ppermute | solution.py:14
  12.5 8.6 %collective-permute-start.1 = (bf16[128,640]{1,0:T(8,128)(2,1)S(1)}, bf16[128,640]{1,0:T(8,128)(2,1)}, u32[]{:S(2)}, u32[]{:S(2)}) collective-permute-start(bf16[128,640]{1,0:T(8,128)(2,1)S(1)} %broadcast_multiply_fusion.1), channel_id=1, source_target_pairs={{16,0},{32,16},{48,32},{64,48},{80,64},{96,80},{112,96},{128,112},... | collective-permute-start | bytes 491528 | tf_op jit(solution)/shard_map/ppermute | solution.py:15
  21.1 0.7 convert_bitcast_fusion.3
  21.7 0.1 mul.53
  21.9 0.0 copy-start
  21.9 2.7 %reshape.31 = bf16[16,16,3072]{2,1,0:T(8,128)(2,1)S(1)} reshape(bf16[16,384,128]{2,1,0:T(8,128)(2,1)} %param.6) | data formatting | bytes 3145728 | tf_op jit(solution)/shard_map/reshape | solution.py:24
  24.6 0.1 broadcast_bitcast_fusion.2
  24.6 0.0 collective-permute-done
  24.6 0.9 slice.20
  25.6 0.0 collective-permute-done.1
  25.6 0.9 slice.21
  26.5 0.0 copy-done
  26.5 3.3 %convert_bitcast_fusion = bf16[16,640,128]{1,2,0:T(8,128)(2,1)} fusion(bf16[16,384,128]{2,1,0:T(8,128)(2,1)S(1)} %copy-done, bf16[384]{0:T(512)(128)(2,1)S(1)} %broadcast_bitcast_fusion.2, bf16[128,512]{1,0:T(8,128)(2,1)S(1)} %slice.21, bf16[128,512]{1,0:T(8,128)(2,1)S(1)} %slice.20, bf16[128,640]{1,0:T(8,128)(2,1)S(1)} %broadcast_multiply_fusion.1), kind=kOutput, calls=%fused_computation.6 | convolution fusion | flops 1011187712 | bytes 4621056 | tf_op jit(solution)/shard_map/ml,pmn->pln/dot_general | solution.py:40
  29.8 1.9 collective-permute-start.2
  31.7 6.0 %collective-permute-start.3 = (bf16[16,640,128]{1,2,0:T(8,128)(2,1)}, bf16[16,640,128]{1,2,0:T(8,128)(2,1)}, u32[]{:S(2)}, u32[]{:S(2)}) collective-permute-start(bf16[16,640,128]{1,2,0:T(8,128)(2,1)} %convert_bitcast_fusion), channel_id=1, source_target_pairs={{16,0},{32,16},{48,32},{64,48},{80,64},{96,80},{112,96},{128,112},... | collective-permute-start | bytes 7864328 | tf_op jit(solution)/shard_map/ppermute | solution.py:15
  37.8 0.1 broadcast_multiply_fusion
  37.9 2.0 copy.19
  39.9 0.0 copy-start.2
  39.9 7.4 %all-to-all-start.1 = ((bf16[16,16,3072]{2,0,1:T(8,128)(2,1)}), bf16[16,16,3072]{2,0,1:T(8,128)(2,1)}, u32[]{:S(2)}, u32[]{:S(2)}) async-start(bf16[16,16,3072]{2,0,1:T(8,128)(2,1)} %copy.19), calls=%async_computation.1 | async-start | bytes 3145728 | tf_op jit(solution)/shard_map/all_to_all | solution.py:59
  47.3 0.0 reduce-scatter.2.cloned.1.call-start
  47.4 0.0 copy-done.2
  47.4 0.1 broadcast_bitcast_fusion.1
  47.5 1.6 slice.23
  49.1 43.4 %collective-permute-done.2 = bf16[16,640,128]{1,2,0:T(8,128)(2,1)} collective-permute-done((bf16[16,640,128]{1,2,0:T(8,128)(2,1)}, bf16[16,640,128]{1,2,0:T(8,128)(2,1)}, u32[]{:S(2)}, u32[]{:S(2)}) %collective-permute-start.2) | collective-permute-done | bytes 2621472 | tf_op jit(solution)/shard_map/ppermute | solution.py:14
  92.5 1.6 slice.22
  94.1 0.0 copy-start.1
  94.1 0.0 collective-permute-done.3
  94.1 1.6 slice.24
  95.7 0.0 copy-done.1
  95.7 1.7 fusion.6
  97.4 0.7 all_to_all.26
  98.1 0.9 copy.18
  99.0 0.0 all-to-all-done.1
  99.0 45.4 %all_to_all.35 = bf16[16,16,3072]{2,0,1:T(8,128)(2,1)S(1)} all-to-all(bf16[16,16,3072]{2,0,1:T(8,128)(2,1)S(1)} %copy.18), channel_id=1, replica_groups=mesh['ao'=32,'ri'=16] {'ri'}, dimensions={1} | all-to-all | bytes 3145728 | tf_op jit(solution)/shard_map/all_to_all | solution.py:58
  144.4 2.7 %fusion.32 = f32[256,256]{1,0:T(8,128)} fusion(bf16[256,3072]{1,0:T(8,128)(2,1)S(1)} %bitcast.29, bf16[256,3072]{1,0:T(8,128)(2,1)} %bitcast.12), kind=kOutput, calls=%fused_computation.39 | convolution fusion | flops 402653184 | bytes 3407872 | tf_op jit(solution)/shard_map/dot_general | solution.py:61
  147.1 0.0 reduce-scatter.2.cloned.1.call-update
  147.2 58.4 %reduce-scatter.2.cloned.1.call-done = f32[16,256]{1,0:T(8,128)} async-done(((f32[256,256]{1,0:T(8,128)}), f32[16,256]{1,0:T(8,128)}) %reduce-scatter.2.cloned.1.call-update) | async-done | bytes 16400 | tf_op jit(solution)/shard_map/reduce_scatter | solution.py:64
  205.6 50.2 %all-gather = f32[512,256]{1,0:T(8,128)S(1)} all-gather(f32[16,256]{1,0:T(8,128)} %reduce-scatter.2.cloned.1.call-done), channel_id=2, replica_groups=mesh['ao'=32,'ri'=16] {'ao'}, dimensions={0}, use_global_device_ids=true | all-gather | bytes 540672 | tf_op jit(solution)/shard_map/all_gather | solution.py:65
  255.9 0.6 neg.3
  (3 shorter events, 0.1 us)
Async XLA Ops:
  8.2 16.4 %collective-permute-start = (bf16[128,640]{1,0:T(8,128)(2,1)S(1)}, bf16[128,640]{1,0:T(8,128)(2,1)}, u32[]{:S(2)}, u32[]{:S(2)}) collective-permute-start(bf16[128,640]{1,0:T(8,128)(2,1)S(1)} %broadcast_multiply_fusion.1), channel_id=1, source_target_pairs={{0,16},{16,32},{32,48},{48,64},{64,80},{80,96},{96,112},{112,128},... | collective-permute-start | bytes 491528 | tf_op jit(solution)/shard_map/ppermute | solution.py:14
  12.5 13.1 %collective-permute-start.1 = (bf16[128,640]{1,0:T(8,128)(2,1)S(1)}, bf16[128,640]{1,0:T(8,128)(2,1)}, u32[]{:S(2)}, u32[]{:S(2)}) collective-permute-start(bf16[128,640]{1,0:T(8,128)(2,1)S(1)} %broadcast_multiply_fusion.1), channel_id=1, source_target_pairs={{16,0},{32,16},{48,32},{64,48},{80,64},{96,80},{112,96},{128,112},... | collective-permute-start | bytes 491528 | tf_op jit(solution)/shard_map/ppermute | solution.py:15
  21.9 4.6 %copy-start = (bf16[16,384,128]{2,1,0:T(8,128)(2,1)S(1)}, bf16[16,384,128]{2,1,0:T(8,128)(2,1)}, u32[]{:S(2)}) copy-start(bf16[16,384,128]{2,1,0:T(8,128)(2,1)} %param.6) | copy-start | bytes 4718596
  29.8 62.6 %collective-permute-start.2 = (bf16[16,640,128]{1,2,0:T(8,128)(2,1)}, bf16[16,640,128]{1,2,0:T(8,128)(2,1)}, u32[]{:S(2)}, u32[]{:S(2)}) collective-permute-start(bf16[16,640,128]{1,2,0:T(8,128)(2,1)} %convert_bitcast_fusion), channel_id=1, source_target_pairs={{0,16},{16,32},{32,48},{48,64},{64,80},{80,96},{96,112},{112,128},... | collective-permute-start | bytes 7864328 | tf_op jit(solution)/shard_map/ppermute | solution.py:14
  31.7 62.3 %collective-permute-start.3 = (bf16[16,640,128]{1,2,0:T(8,128)(2,1)}, bf16[16,640,128]{1,2,0:T(8,128)(2,1)}, u32[]{:S(2)}, u32[]{:S(2)}) collective-permute-start(bf16[16,640,128]{1,2,0:T(8,128)(2,1)} %convert_bitcast_fusion), channel_id=1, source_target_pairs={{16,0},{32,16},{48,32},{64,48},{80,64},{96,80},{112,96},{128,112},... | collective-permute-start | bytes 7864328 | tf_op jit(solution)/shard_map/ppermute | solution.py:15
  39.9 7.4 %copy-start.2 = (s32[1,3]{1,0:T(1,128)S(1)}, s32[1,3]{1,0:T(1,128)}, u32[]{:S(2)}) copy-start(s32[1,3]{1,0:T(1,128)} %param.11) | copy-start | bytes 40
  39.9 59.0 %all-to-all-start.1 = ((bf16[16,16,3072]{2,0,1:T(8,128)(2,1)}), bf16[16,16,3072]{2,0,1:T(8,128)(2,1)}, u32[]{:S(2)}, u32[]{:S(2)}) async-start(bf16[16,16,3072]{2,0,1:T(8,128)(2,1)} %copy.19), calls=%async_computation.1 | async-start | bytes 3145728 | tf_op jit(solution)/shard_map/all_to_all | solution.py:59
  47.3 158.3 %reduce-scatter.2.cloned.1.call-start = ((), (), s32[]{:S(2)}) async-start(), calls=%async_computation.3 | async-start | bytes 278528 | tf_op jit(solution)/shard_map/reduce_scatter | solution.py:64
  94.1 1.7 copy-start.1
Sparse Core Ops, SparseCore 0:
  147.3 58.2 reduce-scatter.1
